TPU v7x, 128 devices: a whole 4x4x4 slice. The times are simulated.
128 devices in a mesh: row: 16 (over z, y), col: 8 (over x, core).
Axes of the slice: x: 4, y: 4, z: 4, core: 2. Of those that a mesh axis runs over, the one named last changes fastest.
Arguments:
- counts: int32 [2048, 262144], P('row', 'col'), may hold values from 0 to 7, as said below
- row_total: float32 [2048], P('row'), may hold values from 1 to 3670016, as said below
- col_total: float32 [262144], P('col'), may hold values from 1 to 3670272, as said below
- grand_total: float32 [1], replicated, as said below
- sketch: float32 [262144, 96], P(('col', 'row')), may hold values from -0.00024414062 to 0.00024414062
Outputs:
- column_factors: float32 [262144, 96], P(('col', 'row'))
- gram_factor: float32 [96, 96], replicated
Inputs may be any that keep to these rules, and one draw needn't show every extreme that they name: About half of the counts are zero. `row_total`: each row's total is its counts' sum times a factor between 1 and 2. `col_total`: each item's total is its counts' sum over the slab plus one, times 262144 / 2048, times a factor between 1 and 2. `grand_total`: the grand total is the sum of col_total times a factor between 1 and 1.25.
All inputs are finite; a program needn't handle non-finite values.
Results may differ from a plain program's by a relative error of at most 0.0003.
Values sent between devices are 32-bit elements; how exact they have to be, the bound alone decides.
No kernel may reach another device: no remote copies, remote signals or barrier semaphores. Data moves between devices by JAX's collectives and lax.ppermute only.
A program may use at most 128 MiB of HBM per device.

v0:
```python
import jax
import jax.numpy as jnp
from jax import lax
from jax.sharding import Mesh
from jax.sharding import PartitionSpec as P

ROW = ("row_0", "row_1")
COL_ROW = ("col", "row_0", "row_1")


def from_everyone(array, axis):
    copies = jnp.broadcast_to(array, (lax.axis_size(axis), *array.shape))
    return lax.all_to_all(copies, axis, split_axis=0, concat_axis=0, tiled=True)


def over_copies(array, axis):
    return from_everyone(array, axis).sum(axis=0)


def over_axes(array, axes):
    for axis in axes:
        array = lax.psum(array, axis)
    return array


def per_device(counts, row_total, col_total, grand_total, sketch):
    row_log = jnp.log(grand_total[0]) - jnp.log(row_total)
    counts_float = counts.astype(jnp.float32)
    pmi = jnp.log(jnp.maximum(counts_float, 1.0)) + row_log[:, None] - jnp.log(col_total)[None, :]
    ppmi_tile = jnp.where(counts > 0, jnp.maximum(pmi, 0.0), 0.0)
    columns = ppmi_tile
    partial_image = jnp.dot(
        columns,
        lax.all_gather(sketch, ROW, axis=0, tiled=True),
        precision=lax.Precision.HIGHEST,
        preferred_element_type=jnp.float32,
    )
    image = over_copies(partial_image, "col")
    gram_local = jnp.dot(
        image.T, image, precision=lax.Precision.HIGHEST, preferred_element_type=jnp.float32
    )
    gram_matrix = over_axes(gram_local, ROW)
    factor = jnp.linalg.cholesky(gram_matrix)
    columns = ppmi_tile
    summed_columns = lax.psum_scatter(
        lax.dot_general(
            columns,
            image,
            (((0,), (0,)), ((), ())),
            precision=lax.Precision.HIGHEST,
            preferred_element_type=jnp.float32,
        ),
        ROW,
        scatter_dimension=0,
        tiled=True,
    )
    column_factors = jax.scipy.linalg.solve_triangular(factor, summed_columns.T, lower=True).T
    return (column_factors, factor)


def solution(mesh):
    finer = Mesh(mesh.devices.reshape(4, 4, mesh.shape["col"]), ("row_0", "row_1", "col"))
    placed = (P(ROW, "col"), P(ROW), P("col"), P(), P(COL_ROW, None))
    return jax.shard_map(
        per_device, mesh=finer, in_specs=placed, out_specs=(P(COL_ROW, None), P()), check_vma=False
    )
```

profile of v0, /device:TPU:1, one launch (start us, length us, event | category | flops | bytes accessed | tf_op | source)
XLA Modules:
  0.0 267.4 jit_solution(10332997755704691555)
XLA Ops:
  7.2 0.0 all-gather.2.cloned.1.call-start
  7.2 0.7 all-gather.2.cloned.1.call-update
  7.9 0.0 reduce-scatter.2.cloned.1.call-start
  7.9 0.9 log.19
  9.6 0.7 log_subtract_fusion
  10.2 92.9 %all-gather.2.cloned.1.call-done = f32[32768,96]{0,1:T(8,128)} async-done(((f32[2048,96]{0,1:T(8,128)}), f32[32768,96]{0,1:T(8,128)}) %all-gather.2.cloned.1.call-update) | async-done | bytes 12582928 | tf_op jit(solution)/shard_map/all_gather | solution.py:34
  103.1 25.3 %fusion.1 = f32[128,96]{0,1:T(8,128)S(1)} fusion(f32[32768,96]{0,1:T(8,128)} %all-gather.2.cloned.1.call-done, s32[128,32768]{1,0:T(8,128)} %param.5, f32[32768]{0:T(1024)S(1)} %log.19, f32[128]{0:T(128)S(1)} %log_subtract_fusion), kind=kOutput, calls=%fused_computation.2 | convolution fusion | flops 4861198336 | bytes 29540864 | tf_op jit(solution)/shard_map/dot_general | solution.py:32
  128.5 12.9 %all_to_all.5 = f32[8,128,96]{1,2,0:T(8,128)S(1)} all-to-all(f32[8,128,96]{1,2,0:T(8,128)S(1)} %broadcast_in_dim.5), channel_id=1, replica_groups=mesh['row_0'=4,'row_1'=4,'col'=8] {'col'}, dimensions={0} | all-to-all | bytes 786432 | tf_op jit(solution)/shard_map/all_to_all | solution.py:13
  141.4 23.0 %fusion = f32[32768,96]{0,1:T(8,128)} fusion(f32[128,96]{0,1:T(8,128)S(1)} %reduce_sum.9, s32[128,32768]{1,0:T(8,128)} %param.5, f32[32768]{0:T(1024)S(1)} %log.19, f32[128]{0:T(128)S(1)} %log_subtract_fusion), kind=kOutput, calls=%fused_computation.1 | convolution fusion | flops 4861198336 | bytes 29540864 | tf_op jit(solution)/shard_map/dot_general | solution.py:46
  164.4 0.0 reduce-scatter.2.cloned.1.call-update
  164.4 0.2 fusion.21
  164.7 15.1 %psum.14 = f32[96,96]{0,1:T(8,128)S(1)} all-reduce(f32[96,96]{0,1:T(8,128)S(1)} %fusion.21), channel_id=1, replica_groups=mesh['row_0'=4,'row_1'=4,'col'=8] {'row_0'}, use_global_device_ids=true, to_apply=%region_2.3 | all-reduce | flops 9216 | bytes 73728 | tf_op jit(solution)/shard_map/psum | solution.py:22
  179.7 13.8 %psum.15 = f32[96,96]{0,1:T(8,128)S(1)} all-reduce(f32[96,96]{0,1:T(8,128)S(1)} %psum.14), channel_id=1, replica_groups=mesh['row_0'=4,'row_1'=4,'col'=8] {'row_1'}, use_global_device_ids=true, to_apply=%region_3.4 | all-reduce | flops 9216 | bytes 73728 | tf_op jit(solution)/shard_map/psum | solution.py:22
  193.6 0.1 copy.13
  193.7 8.8 %cholesky.16 = f32[96,96]{1,0:T(8,128)S(1)} custom-call(f32[96,96]{1,0:T(8,128)S(1)} %fusion.14), custom_call_target="Cholesky" | custom-call | tf_op jit(solution)/shard_map/jit(cholesky)/cholesky | solution.py:43
  202.5 0.6 compare_reduce_fusion
  203.1 1.3 select_bitcast_fusion
  204.4 7.4 %custom-call.7 = f32[1,96,96]{1,2,0:T(8,128)S(1)} custom-call(f32[1,96,96]{2,1,0:T(8,128)S(1)} %get-tuple-element.2), custom_call_target="InvertDiagBlocksLowerTriangular" | custom-call | tf_op jit(solution)/shard_map/jit(_solve_triangular)/triangular_solve | solution.py:57
  211.8 46.0 %reduce-scatter.2.cloned.1.call-done = f32[2048,96]{0,1:T(8,128)} async-done(((f32[32768,96]{0,1:T(8,128)}), f32[2048,96]{0,1:T(8,128)}) %reduce-scatter.2.cloned.1.call-update) | async-done | bytes 786448 | tf_op jit(solution)/shard_map/reduce_scatter | solution.py:45
  257.8 2.8 %fusion.12 = f32[2048,96]{0,1:T(8,128)} fusion(f32[2048,96]{0,1:T(8,128)} %reduce-scatter.2.cloned.1.call-done, f32[1,96,96]{1,2,0:T(8,128)S(1)} %custom-call.7), kind=kOutput, calls=%fused_computation.13 | convolution fusion | flops 226492416 | bytes 1609728 | tf_op jit(solution)/shard_map/jit(_solve_triangular)/triangular_solve | solution.py:57
  (4 shorter events, 0.1 us)
Async XLA Ops:
  7.2 95.9 %all-gather.2.cloned.1.call-start = ((), (), s32[]{:S(2)}) async-start(), calls=%async_computation.2 | async-start | bytes 13369344 | tf_op jit(solution)/shard_map/all_gather | solution.py:34
  7.9 249.9 %reduce-scatter.2.cloned.1.call-start = ((), (), s32[]{:S(2)}) async-start(), calls=%async_computation.3 | async-start | bytes 13369344 | tf_op jit(solution)/shard_map/reduce_scatter | solution.py:45
Sparse Core Ops, SparseCore 0:
  10.1 92.9 all-gather.1
  164.5 93.1 reduce-scatter.1
where the time goes:
time: 268 us; the launch traced here: 267 us
  waiting for transfers between devices  140 us (52%)
  matrix products  51.3 us (19%)
  blocking collectives  41.8 us (16%)
  other arithmetic  18.8 us (7%)
  between operations  14.8 us (6%)
    all_gather x1, waiting for transfers between devices, per_device(): lax.all_gather(sketch, ROW, axis=0, tiled=True)  92.9 us
    reduce_scatter x1, waiting for transfers between devices, per_device(): lax.psum_scatter(lax.dot_general(columns, image, (((0,), (0,)), ((), ()))...  46 us
    psum x2, blocking collectives, over_axes(): array = lax.psum(array, axis)  28.9 us
    dot_general x1, matrix products, per_device(): jnp.dot(columns, lax.all_gather(sketch, ROW, axis=0, tiled=True), precisi...  25.3 us
    dot_general x1, matrix products, per_device(): lax.dot_general(columns, image, (((0,), (0,)), ((), ())), precision=lax.P...  23 us
    all_to_all x1, blocking collectives, from_everyone(): return lax.all_to_all(copies, axis, split_axis=0, concat_axis=0, tiled=True)  12.9 us
    another operation x3, other arithmetic, per_device(): factor = jnp.linalg.cholesky(gram_matrix)  9.45 us
    another operation x2, other arithmetic, per_device(): jax.scipy.linalg.solve_triangular(factor, summed_columns.T, lower=True)  8.63 us
  transfers between devices with their start and end apart: 2, of which 2 were waited for; matrix products, arithmetic and copies ran while one was open for 7% of the time, Pallas kernels for 0%

commit v1 on v0

--- a/solution.py
+++ b/solution.py
@@ -19,7 +19,8 @@
 
 def over_axes(array, axes):
     for axis in axes:
-        array = lax.psum(array, axis)
+        parts = lax.all_gather(array, axis)
+        array = jnp.sum(parts, axis=0)
     return array
 
 

time: 268 us -> 268 us (level)
  waiting for transfers between devices: 140 us -> 148 us
  blocking collectives: 41.8 us -> 34.1 us
    psum x2 -> x0, blocking collectives: 28.9 us -> none  [over_axes(): array = lax.psum(array, axis)]
    all_gather x0 -> x2, blocking collectives: none -> 21.2 us  [over_axes(): parts = lax.all_gather(array, axis)]
    reduce_scatter x1, waiting for transfers between devices: 46 us -> 54.2 us  [per_device(): lax.psum_scatter(lax.dot_general(columns, image, (((0,), (0,)), ((), ()))...]
where the time goes in v1:
time: 268 us
  waiting for transfers between devices  148 us (55%)
  matrix products  51.3 us (19%)
  blocking collectives  34.1 us (13%)
  other arithmetic  18.8 us (7%)
  between operations  14.8 us (6%)
    all_gather x1, waiting for transfers between devices, per_device(): lax.all_gather(sketch, ROW, axis=0, tiled=True)  92.9 us
    reduce_scatter x1, waiting for transfers between devices, per_device(): lax.psum_scatter(lax.dot_general(columns, image, (((0,), (0,)), ((), ()))...  54.2 us
    dot_general x1, matrix products, per_device(): jnp.dot(columns, lax.all_gather(sketch, ROW, axis=0, tiled=True), precisi...  25.3 us
    dot_general x1, matrix products, per_device(): lax.dot_general(columns, image, (((0,), (0,)), ((), ())), precision=lax.P...  23 us
    all_gather x2, blocking collectives, over_axes(): parts = lax.all_gather(array, axis)  21.2 us
    all_to_all x1, blocking collectives, from_everyone(): return lax.all_to_all(copies, axis, split_axis=0, concat_axis=0, tiled=True)  12.9 us
    another operation x3, other arithmetic, per_device(): factor = jnp.linalg.cholesky(gram_matrix)  9.45 us
    another operation x2, other arithmetic, per_device(): jax.scipy.linalg.solve_triangular(factor, summed_columns.T, lower=True)  8.63 us
  transfers between devices with their start and end apart: 2, of which 2 were waited for; matrix products, arithmetic and copies ran while one was open for 7% of the time, Pallas kernels for 0%

profile of v1, /device:TPU:1, one launch (start us, length us, event | category | flops | bytes accessed | tf_op | source)
XLA Modules:
  0.0 267.9 jit_solution(2486787197261087222)
XLA Ops:
  7.2 0.0 all-gather.4.cloned.1.call-start
  7.2 0.7 all-gather.4.cloned.1.call-update
  7.9 0.0 reduce-scatter.2.cloned.1.call-start
  7.9 0.9 log.19
  9.6 0.7 log_subtract_fusion
  10.2 92.9 %all-gather.4.cloned.1.call-done = f32[32768,96]{0,1:T(8,128)} async-done(((f32[2048,96]{0,1:T(8,128)}), f32[32768,96]{0,1:T(8,128)}) %all-gather.4.cloned.1.call-update) | async-done | bytes 12582928 | tf_op jit(solution)/shard_map/all_gather | solution.py:35
  103.1 25.3 %fusion.1 = f32[128,96]{0,1:T(8,128)S(1)} fusion(f32[32768,96]{0,1:T(8,128)} %all-gather.4.cloned.1.call-done, s32[128,32768]{1,0:T(8,128)} %param.5, f32[32768]{0:T(1024)S(1)} %log.19, f32[128]{0:T(128)S(1)} %log_subtract_fusion), kind=kOutput, calls=%fused_computation.2 | convolution fusion | flops 4861198336 | bytes 29540864 | tf_op jit(solution)/shard_map/dot_general | solution.py:33
  128.5 12.9 %all_to_all.5 = f32[8,128,96]{1,2,0:T(8,128)S(1)} all-to-all(f32[8,128,96]{1,2,0:T(8,128)S(1)} %broadcast_in_dim.5), channel_id=1, replica_groups=mesh['row_0'=4,'row_1'=4,'col'=8] {'col'}, dimensions={0} | all-to-all | bytes 786432 | tf_op jit(solution)/shard_map/all_to_all | solution.py:13
  141.4 23.0 %fusion = f32[32768,96]{0,1:T(8,128)} fusion(f32[128,96]{0,1:T(8,128)S(1)} %reduce_sum.27, s32[128,32768]{1,0:T(8,128)} %param.5, f32[32768]{0:T(1024)S(1)} %log.19, f32[128]{0:T(128)S(1)} %log_subtract_fusion), kind=kOutput, calls=%fused_computation.1 | convolution fusion | flops 4861198336 | bytes 29540864 | tf_op jit(solution)/shard_map/dot_general | solution.py:47
  164.4 0.0 reduce-scatter.2.cloned.1.call-update
  164.4 0.2 fusion.21
  164.7 9.8 %all-gather = f32[384,96]{1,0:T(8,128)S(1)} all-gather(f32[96,96]{1,0:T(8,128)S(1)} %fusion.21), channel_id=2, replica_groups=mesh['row_0'=4,'row_1'=4,'col'=8] {'row_0'}, dimensions={0}, use_global_device_ids=true | all-gather | bytes 184320 | tf_op jit(solution)/shard_map/all_gather | solution.py:22
  174.5 11.3 %all-gather.1 = f32[384,96]{1,0:T(8,128)S(1)} all-gather(f32[96,96]{1,0:T(8,128)S(1)} %reduce_sum.28), channel_id=3, replica_groups=mesh['row_0'=4,'row_1'=4,'col'=8] {'row_1'}, dimensions={0}, use_global_device_ids=true | all-gather | bytes 184320 | tf_op jit(solution)/shard_map/all_gather | solution.py:22
  185.9 0.1 copy.11
  186.0 8.8 %cholesky.16 = f32[96,96]{1,0:T(8,128)S(1)} custom-call(f32[96,96]{1,0:T(8,128)S(1)} %fusion.14), custom_call_target="Cholesky" | custom-call | tf_op jit(solution)/shard_map/jit(cholesky)/cholesky | solution.py:44
  194.8 0.6 compare_reduce_fusion
  195.4 1.3 select_bitcast_fusion
  196.7 7.4 %custom-call.7 = f32[1,96,96]{1,2,0:T(8,128)S(1)} custom-call(f32[1,96,96]{2,1,0:T(8,128)S(1)} %get-tuple-element.2), custom_call_target="InvertDiagBlocksLowerTriangular" | custom-call | tf_op jit(solution)/shard_map/jit(_solve_triangular)/triangular_solve | solution.py:58
  204.1 54.2 %reduce-scatter.2.cloned.1.call-done = f32[2048,96]{0,1:T(8,128)} async-done(((f32[32768,96]{0,1:T(8,128)}), f32[2048,96]{0,1:T(8,128)}) %reduce-scatter.2.cloned.1.call-update) | async-done | bytes 786448 | tf_op jit(solution)/shard_map/reduce_scatter | solution.py:46
  258.2 2.8 %fusion.12 = f32[2048,96]{0,1:T(8,128)} fusion(f32[2048,96]{0,1:T(8,128)} %reduce-scatter.2.cloned.1.call-done, f32[1,96,96]{1,2,0:T(8,128)S(1)} %custom-call.7), kind=kOutput, calls=%fused_computation.13 | convolution fusion | flops 226492416 | bytes 1609728 | tf_op jit(solution)/shard_map/jit(_solve_triangular)/triangular_solve | solution.py:58
  (6 shorter events, 0.1 us)
Async XLA Ops:
  7.2 95.9 %all-gather.4.cloned.1.call-start = ((), (), s32[]{:S(2)}) async-start(), calls=%async_computation.2 | async-start | bytes 13369344 | tf_op jit(solution)/shard_map/all_gather | solution.py:35
  7.9 250.3 %reduce-scatter.2.cloned.1.call-start = ((), (), s32[]{:S(2)}) async-start(), calls=%async_computation.3 | async-start | bytes 13369344 | tf_op jit(solution)/shard_map/reduce_scatter | solution.py:46
Sparse Core Ops, SparseCore 0:
  10.1 92.9 all-gather.3
  164.5 93.6 reduce-scatter.1

commit v2 on v0

--- a/solution.py
+++ b/solution.py
@@ -6,6 +6,12 @@
 
 ROW = ("row_0", "row_1")
 COL_ROW = ("col", "row_0", "row_1")
+
+
+def balance_lots_all(array_here):
+    return jnp.concatenate(
+        lax.all_to_all(jnp.stack(lax.psum(1, ROW) * [array_here], axis=0), ROW, 0, 0), axis=0
+    )
 
 
 def from_everyone(array, axis):
@@ -31,7 +37,7 @@
     columns = ppmi_tile
     partial_image = jnp.dot(
         columns,
-        lax.all_gather(sketch, ROW, axis=0, tiled=True),
+        balance_lots_all(sketch),
         precision=lax.Precision.HIGHEST,
         preferred_element_type=jnp.float32,
     )

time: 268 us -> 386 us (1.44)
  waiting for transfers between devices: 140 us -> 233 us
  local copies, waits for them, and re-layouts: 1.04 us -> 18.6 us
  starting transfers between devices: 0.08 us -> 8.67 us
    all_to_all x0 -> x1, waiting for transfers between devices: none -> 185 us  [balance_lots_all(): lax.all_to_all(jnp.stack(lax.psum(1, ROW) * [array_here], axis=0), ROW, 0...]
    all_gather x1 -> x0, waiting for transfers between devices: 92.9 us -> none  [per_device(): lax.all_gather(sketch, ROW, axis=0, tiled=True)]
    reshape x0 -> x1, local copies, waits for them, and re-layouts: none -> 11.2 us  [balance_lots_all(): jnp.concatenate(lax.all_to_all(jnp.stack(lax.psum(1, ROW) * [array_here],...]
    all_to_all x0 -> x1, starting transfers between devices: none -> 8.63 us  [balance_lots_all(): lax.all_to_all(jnp.stack(lax.psum(1, ROW) * [array_here], axis=0), ROW, 0...]
    another operation x0 -> x1, local copies, waits for them, and re-layouts: none -> 7.23 us  [balance_lots_all(): jnp.stack(lax.psum(1, ROW) * [array_here], axis=0)]
  transfers between devices with their start and end apart: 2 -> 2, of which waited for: 2 -> 2; matrix products, arithmetic and copies ran while one was open for 7% -> 5% of each run, Pallas kernels for 0% -> 0%
where the time goes in v2:
time: 386 us; the launch traced here: 385 us
  waiting for transfers between devices  233 us (60%)
  matrix products  51.3 us (13%)
  blocking collectives  40.8 us (11%)
  local copies, waits for them, and re-layouts  18.6 us (5%)
  other arithmetic  18.1 us (5%)
  between operations  14.8 us (4%)
  starting transfers between devices  8.67 us (2%)
    all_to_all x1, waiting for transfers between devices, balance_lots_all(): lax.all_to_all(jnp.stack(lax.psum(1, ROW) * [array_here], axis=0), ROW, 0...  185 us
    reduce_scatter x1, waiting for transfers between devices, per_device(): lax.psum_scatter(lax.dot_general(columns, image, (((0,), (0,)), ((), ()))...  47.4 us
    psum x2, blocking collectives, over_axes(): array = lax.psum(array, axis)  26.9 us
    dot_general x1, matrix products, per_device(): jnp.dot(columns, balance_lots_all(sketch), precision=lax.Precision.HIGHES...  25.3 us
    dot_general x1, matrix products, per_device(): lax.dot_general(columns, image, (((0,), (0,)), ((), ())), precision=lax.P...  23 us
    all_to_all x1, blocking collectives, from_everyone(): return lax.all_to_all(copies, axis, split_axis=0, concat_axis=0, tiled=True)  13.9 us
    reshape x1, local copies, waits for them, and re-layouts, balance_lots_all(): jnp.concatenate(lax.all_to_all(jnp.stack(lax.psum(1, ROW) * [array_here],...  11.2 us
    another operation x3, other arithmetic, per_device(): factor = jnp.linalg.cholesky(gram_matrix)  9.45 us
  transfers between devices with their start and end apart: 2, of which 2 were waited for; matrix products, arithmetic and copies ran while one was open for 5% of the time, Pallas kernels for 0%

profile of v2, /device:TPU:1, one launch (start us, length us, event | category | flops | bytes accessed | tf_op | source)
XLA Modules:
  0.0 385.3 jit_solution(11962269980898573478)
XLA Ops:
  7.2 0.0 copy-start
  7.2 0.0 copy-start.1
  7.2 7.2 %stack.2 = f32[16,2048,96]{1,2,0:T(8,128)} broadcast(f32[2048,96]{0,1:T(8,128)} %param.9), dimensions={1,2} | broadcast | bytes 13369344 | tf_op jit(solution)/shard_map/stack | solution.py:13
  14.4 8.6 %all-to-all-start = ((f32[16,2048,96]{1,2,0:T(8,128)}), f32[16,2048,96]{1,2,0:T(8,128)}, u32[]{:S(2)}, u32[]{:S(2)}) async-start(f32[16,2048,96]{1,2,0:T(8,128)} %stack.2), calls=%async_computation | async-start | bytes 25165824 | tf_op jit(solution)/shard_map/all_to_all | solution.py:13
  23.0 0.0 reduce-scatter.2.cloned.1.call-start
  23.1 0.0 copy-done
  23.8 0.0 copy-done.1
  23.9 185.4 %all-to-all-done = f32[16,2048,96]{1,2,0:T(8,128)} async-done(((f32[16,2048,96]{1,2,0:T(8,128)}), f32[16,2048,96]{1,2,0:T(8,128)}, u32[]{:S(2)}, u32[]{:S(2)}) %all-to-all-start) | async-done | bytes 12582944 | tf_op jit(solution)/shard_map/all_to_all | solution.py:13
  209.3 11.2 %copy.20 = f32[16,12,8,2048]{3,2,0,1:T(8,128)} copy(f32[16,12,8,2048]{3,2,1,0:T(8,128)} %bitcast.4) | data formatting | bytes 25165824 | tf_op jit(solution)/shard_map/reshape | solution.py:12
  220.5 25.3 %fusion.1 = f32[128,96]{0,1:T(8,128)S(1)} fusion(f32[32768,96]{0,1:T(8,128)} %bitcast.17, s32[128,32768]{1,0:T(8,128)} %param.5, f32[32768]{0:T(1024)S(1)} %log.19, f32[128]{0:T(128)S(1)} %log_subtract_fusion), kind=kOutput, calls=%fused_computation.2 | convolution fusion | flops 4861198336 | bytes 29540864 | tf_op jit(solution)/shard_map/dot_general | solution.py:38
  245.9 13.9 %all_to_all.10 = f32[8,128,96]{1,2,0:T(8,128)S(1)} all-to-all(f32[8,128,96]{1,2,0:T(8,128)S(1)} %broadcast_in_dim.5), channel_id=1, replica_groups=mesh['row_0'=4,'row_1'=4,'col'=8] {'col'}, dimensions={0} | all-to-all | bytes 786432 | tf_op jit(solution)/shard_map/all_to_all | solution.py:19
  259.8 23.0 %fusion = f32[32768,96]{0,1:T(8,128)} fusion(f32[128,96]{0,1:T(8,128)S(1)} %reduce_sum.9, s32[128,32768]{1,0:T(8,128)} %param.5, f32[32768]{0:T(1024)S(1)} %log.19, f32[128]{0:T(128)S(1)} %log_subtract_fusion), kind=kOutput, calls=%fused_computation.1 | convolution fusion | flops 4861198336 | bytes 29540864 | tf_op jit(solution)/shard_map/dot_general | solution.py:52
  282.8 0.0 reduce-scatter.2.cloned.1.call-update
  282.8 0.2 fusion.21
  283.0 13.4 %psum.14 = f32[96,96]{0,1:T(8,128)S(1)} all-reduce(f32[96,96]{0,1:T(8,128)S(1)} %fusion.21), channel_id=1, replica_groups=mesh['row_0'=4,'row_1'=4,'col'=8] {'row_0'}, use_global_device_ids=true, to_apply=%region_2.3 | all-reduce | flops 9216 | bytes 73728 | tf_op jit(solution)/shard_map/psum | solution.py:28
  296.4 13.5 %psum.15 = f32[96,96]{0,1:T(8,128)S(1)} all-reduce(f32[96,96]{0,1:T(8,128)S(1)} %psum.14), channel_id=1, replica_groups=mesh['row_0'=4,'row_1'=4,'col'=8] {'row_1'}, use_global_device_ids=true, to_apply=%region_3.4 | all-reduce | flops 9216 | bytes 73728 | tf_op jit(solution)/shard_map/psum | solution.py:28
  309.9 0.1 copy.18
  310.0 8.8 %cholesky.16 = f32[96,96]{1,0:T(8,128)S(1)} custom-call(f32[96,96]{1,0:T(8,128)S(1)} %fusion.14), custom_call_target="Cholesky" | custom-call | tf_op jit(solution)/shard_map/jit(cholesky)/cholesky | solution.py:49
  318.8 0.6 compare_reduce_fusion
  319.5 1.3 select_bitcast_fusion
  320.8 7.4 %custom-call.7 = f32[1,96,96]{1,2,0:T(8,128)S(1)} custom-call(f32[1,96,96]{2,1,0:T(8,128)S(1)} %get-tuple-element.2), custom_call_target="InvertDiagBlocksLowerTriangular" | custom-call | tf_op jit(solution)/shard_map/jit(_solve_triangular)/triangular_solve | solution.py:63
  328.1 47.4 %reduce-scatter.2.cloned.1.call-done = f32[2048,96]{0,1:T(8,128)} async-done(((f32[32768,96]{0,1:T(8,128)}), f32[2048,96]{0,1:T(8,128)}) %reduce-scatter.2.cloned.1.call-update) | async-done | bytes 786448 | tf_op jit(solution)/shard_map/reduce_scatter | solution.py:51
  375.6 2.8 fusion.12
  (6 shorter events, 0.1 us)
Async XLA Ops:
  7.2 15.9 %copy-start = (f32[32768]{0:T(1024)S(1)}, f32[32768]{0:T(1024)}, u32[]{:S(2)}) copy-start(f32[32768]{0:T(1024)} %param.7) | copy-start | bytes 393220
  7.2 16.7 %copy-start.1 = (f32[128]{0:T(128)S(1)}, f32[128]{0:T(128)}, u32[]{:S(2)}) copy-start(f32[128]{0:T(128)} %param.6) | copy-start | bytes 1540
  14.4 194.9 %all-to-all-start = ((f32[16,2048,96]{1,2,0:T(8,128)}), f32[16,2048,96]{1,2,0:T(8,128)}, u32[]{:S(2)}, u32[]{:S(2)}) async-start(f32[16,2048,96]{1,2,0:T(8,128)} %stack.2), calls=%async_computation | async-start | bytes 25165824 | tf_op jit(solution)/shard_map/all_to_all | solution.py:13
  23.0 352.5 %reduce-scatter.2.cloned.1.call-start = ((), (), s32[]{:S(2)}) async-start(), calls=%async_computation.3 | async-start | bytes 13369344 | tf_op jit(solution)/shard_map/reduce_scatter | solution.py:51
Sparse Core Ops, SparseCore 0:
  282.9 92.6 reduce-scatter.1
